TPU v7x, 512 devices: a whole 4x4x16 slice. The times are simulated.
512 devices in a mesh: grp: 16 (over y, x), tok: 32 (over z, core).
Axes of the slice: x: 4, y: 4, z: 16, core: 2. Of those that a mesh axis runs over, the one named last changes fastest.
Arguments:
- hidden_in: bfloat16 [16, 4096, 1024], P('grp', 'tok'), may hold values from -6 to 6
- lengths: int32 [16, 3], P('grp'), may hold values from 1 to 3072, 4096 in all within a row
- prefix_cache: bfloat16 [16, 512, 512], P('grp', 'tok'), may hold values from -2600 to 2600
- routes: int32 [16, 4096, 8], P('grp', 'tok'), may hold values from 0 to 31, all different within a row; in each aligned block of 128 rows (0 to 127, 128 to 255, ..., all dimensions but the last counted through in order) at most 40 rows name the same one
- gates: float32 [16, 4096, 8], P('grp', 'tok'), may hold values from 0.05 to 0.4
- attn_gain: float32 [1024], replicated, may hold values from 0.1 to 1.9
- w_qkv: bfloat16 [1024, 1024], P('grp', 'tok'), may hold values from -0.75 to 0.75
- w_out: bfloat16 [512, 1024], P('grp', 'tok'), may hold values from -0.25 to 0.25
- moe_gain: float32 [1024], replicated, may hold values from 0.1 to 1.9
- expert_gate_up: bfloat16 [32, 1024, 1024], P('tok', 'grp'), may hold values from -0.1875 to 0.1875
- expert_down: bfloat16 [32, 512, 1024], P('tok', 'grp'), may hold values from -0.25 to 0.25
Outputs:
- hidden_out: bfloat16 [16, 4096, 1024], P('grp', 'tok')
- suffix_cache: bfloat16 [16, 4096, 512], P('grp', 'tok')
Inputs may be any that keep to these rules, and one draw needn't show every extreme that they name: Each group's 3 lengths sum to 4096; no request is longer than 3072 tokens, and some request of every draw has exactly 3072. `routes`: each token names 8 different experts. Among the 128 tokens of one device no expert is named more than 40 times, a bound that some block reaches.
All inputs are finite; a program needn't handle non-finite values.
Results may differ from a plain program's by a relative error of at most 0.02.
Values may be sent and summed in bfloat16 or wider, within the bound.
A program may use at most 128 MiB of HBM per device.

v0:
```python
import jax
import jax.numpy as jnp
from jax import lax
from jax.sharding import PartitionSpec as P

HEADS = 8
KV_HEADS = 4
HEAD_DIM = 64
FF = 512
EXPERTS = 32
TOP = 8
CAP = 40
epsilon = 1e-05
score_scale = 0.015625
rope_base = 10000.0
big_negative = -1e30


def rms_scale(values, gain):
    values = values.astype(jnp.float32)
    mean_square = jnp.mean(values * values, axis=-1, keepdims=True)
    return values * lax.rsqrt(mean_square + epsilon) * gain


def request_layout(group_lengths, token_index):
    ends = jnp.cumsum(group_lengths)
    starts = ends - group_lengths
    segment = jnp.sum((token_index[:, None] >= ends[None, :]).astype(jnp.int32), axis=1)
    match = segment[:, None] == jnp.arange(group_lengths.shape[0], dtype=jnp.int32)[None, :]
    offset = token_index - jnp.sum(jnp.where(match, starts[None, :], 0), axis=1)
    return (segment, offset)


def rotate(values, position):
    half_width = values.shape[-1] // 2
    frequency = rope_base ** (-jnp.arange(half_width, dtype=jnp.float32) * 2.0 / values.shape[-1])
    angle = position.astype(jnp.float32)[:, None] * frequency[None, :]
    cosine = jnp.cos(angle)[:, None, :]
    sine = jnp.sin(angle)[:, None, :]
    first = values[..., :half_width]
    second = values[..., half_width:]
    return jnp.concatenate(
        [first * cosine - second * sine, second * cosine + first * sine], axis=-1
    )


def gather_small(blocks):
    flat = jnp.concatenate([b.reshape(-1) for b in blocks])
    gathered = lax.all_gather(flat[None], "tok", axis=0, tiled=True)
    pieces, start = ([], 0)
    for b in blocks:
        size = b.size
        pieces.append(gathered[:, start : start + size].reshape((-1,) + b.shape[1:]))
        start += size
    return pieces


def gather_rows(by_columns):
    return lax.all_gather(by_columns[None], "grp", axis=0, tiled=True)


def attend(carry, grouped, keys_values, allowed):
    best, total, mixed = carry
    key_count = keys_values.shape[0]
    key_width = KV_HEADS * HEAD_DIM
    key_heads = keys_values[:, :key_width].reshape(key_count, KV_HEADS, HEAD_DIM).transpose(1, 0, 2)
    value_heads = (
        keys_values[:, key_width:].reshape(key_count, KV_HEADS, HEAD_DIM).transpose(1, 0, 2)
    )
    scores = (
        jnp.einsum("kqd,knd->kqn", grouped, key_heads, preferred_element_type=jnp.float32)
        * score_scale
    )
    if allowed is not None:
        row_count = grouped.shape[1]
        share = row_count // allowed.shape[0]
        mask = jnp.broadcast_to(allowed[:, None, :], (allowed.shape[0], share, key_count)).reshape(
            row_count, key_count
        )
        scores = jnp.where(mask[None], scores, big_negative)
    new_best = jnp.maximum(best, jnp.max(scores, axis=-1))
    factor = jnp.exp(best - new_best)
    probs = jnp.exp(scores - new_best[..., None])
    total = total * factor + jnp.sum(probs, axis=-1)
    mixed = mixed * factor[..., None] + jnp.einsum(
        "kqn,knd->kqd", probs.astype(jnp.bfloat16), value_heads, preferred_element_type=jnp.float32
    )
    return (new_best, total, mixed)


def local(
    hidden_in,
    lengths,
    prefix_cache,
    routes,
    gates,
    attn_gain,
    w_qkv,
    w_out,
    moe_gain,
    expert_gate_up,
    expert_down,
):
    tokens_here = hidden_in[0]
    tok_count = tokens_here.shape[0]
    axis_count = lax.axis_size("tok")
    device_place = lax.axis_index("tok")
    group_lengths = lengths[0]
    token_index = device_place * tok_count + jnp.arange(tok_count, dtype=jnp.int32)
    segment, offset = request_layout(group_lengths, token_index)
    position = prefix_cache.shape[1] * axis_count + offset
    query_width = HEADS * HEAD_DIM
    key_width = KV_HEADS * HEAD_DIM
    group_share = HEADS // KV_HEADS
    normed = rms_scale(tokens_here, attn_gain).astype(jnp.bfloat16)
    qkv_columns, out_columns, prefix_all = gather_small([w_qkv.T, w_out.T, prefix_cache[0]])
    qkv_weight = gather_rows(qkv_columns)
    projected = jnp.einsum(
        "ngr,gcr->nc",
        normed.reshape(tok_count, qkv_weight.shape[0], qkv_weight.shape[2]),
        qkv_weight,
        preferred_element_type=jnp.float32,
    )
    query = rotate(projected[:, :query_width].reshape(tok_count, HEADS, HEAD_DIM), position).astype(
        jnp.bfloat16
    )
    keys_new = rotate(
        projected[:, query_width : query_width + key_width].reshape(tok_count, KV_HEADS, HEAD_DIM),
        position,
    ).astype(jnp.bfloat16)
    values_new = projected[:, query_width + key_width :].astype(jnp.bfloat16)
    suffix_cache = jnp.concatenate([keys_new.reshape(tok_count, key_width), values_new], axis=1)
    row_count = tok_count * group_share
    grouped = (
        query.reshape(tok_count, KV_HEADS, group_share, HEAD_DIM)
        .transpose(1, 0, 2, 3)
        .reshape(KV_HEADS, row_count, HEAD_DIM)
    )
    start_carry = (
        jnp.full((KV_HEADS, row_count), big_negative, jnp.float32),
        jnp.zeros((KV_HEADS, row_count), jnp.float32),
        jnp.zeros((KV_HEADS, row_count, HEAD_DIM), jnp.float32),
    )
    carry = attend(start_carry, grouped, prefix_all, None)
    piece = lax.all_gather(suffix_cache, "tok", axis=0, tiled=True)
    key_index = jnp.arange(piece.shape[0], dtype=jnp.int32)
    key_segment, key_offset = request_layout(group_lengths, key_index)
    earlier = key_index[None, :] <= token_index[:, None]
    same_request = key_segment[None, :] == segment[:, None]
    carry = attend(carry, grouped, piece, earlier & same_request & (key_index[None, :] >= 0))
    best, total, mixed = carry
    attended = (mixed / total[..., None]).reshape(KV_HEADS, tok_count, group_share, HEAD_DIM)
    attended = attended.transpose(1, 0, 2, 3).reshape(tok_count, query_width).astype(jnp.bfloat16)
    out_weight = gather_rows(out_columns)
    projected_out = jnp.einsum(
        "ngr,gcr->nc",
        attended.reshape(tok_count, out_weight.shape[0], out_weight.shape[2]),
        out_weight,
        preferred_element_type=jnp.float32,
    )
    after_attention = tokens_here.astype(jnp.float32) + projected_out
    moe_in = rms_scale(after_attention, moe_gain).astype(jnp.bfloat16)
    model_width = moe_in.shape[1]
    flat_routes = routes[0].reshape(-1)
    onehot = (flat_routes[:, None] == jnp.arange(EXPERTS, dtype=jnp.int32)[None, :]).astype(
        jnp.int32
    )
    slot_rank = jnp.sum(jnp.cumsum(onehot, axis=0) * onehot, axis=1) - 1
    slot_index = flat_routes * CAP + slot_rank
    source_token = jnp.arange(flat_routes.shape[0], dtype=jnp.int32) // TOP
    outgoing = (
        jnp.zeros((EXPERTS * CAP, model_width), jnp.bfloat16)
        .at[slot_index]
        .set(moe_in[source_token])
    )
    arrived = lax.all_to_all(
        outgoing.reshape(EXPERTS, CAP, model_width), "tok", split_axis=0, concat_axis=0, tiled=True
    ).reshape(1, EXPERTS * CAP, model_width)
    sliced = arrived
    hidden_pair = jnp.einsum(
        "erd,edf->erf",
        sliced,
        lax.all_gather(expert_gate_up, "grp", axis=1, tiled=True),
        preferred_element_type=jnp.float32,
    )
    activated = (jax.nn.silu(hidden_pair[..., :FF]) * hidden_pair[..., FF:]).astype(jnp.bfloat16)
    sliced = activated
    expert_result = jnp.einsum(
        "erf,efd->erd",
        sliced,
        lax.all_gather(expert_down, "grp", axis=1, tiled=True),
        preferred_element_type=jnp.float32,
    ).astype(jnp.bfloat16)
    returned = lax.all_to_all(
        expert_result.reshape(EXPERTS, CAP, model_width),
        "tok",
        split_axis=0,
        concat_axis=0,
        tiled=True,
    ).reshape(EXPERTS * CAP, -1)
    weighted = returned[slot_index].astype(jnp.float32) * gates[0].reshape(-1)[:, None]
    moe_out = jnp.sum(weighted.reshape(tok_count, TOP, -1), axis=1)
    hidden_out = (after_attention + moe_out).astype(jnp.bfloat16)
    return (hidden_out[None], suffix_cache[None])


def solution(mesh):
    return jax.shard_map(
        local,
        mesh=mesh,
        in_specs=(
            P("grp", "tok", None),
            P("grp", None),
            P("grp", "tok", None),
            P("grp", "tok", None),
            P("grp", "tok", None),
            P(),
            P("grp", "tok"),
            P("grp", "tok"),
            P(),
            P("tok", "grp", None),
            P("tok", "grp", None),
        ),
        out_specs=(P("grp", "tok", None), P("grp", "tok", None)),
        check_vma=False,
    )
```

profile of v0, /device:TPU:32, one launch (start us, length us, event | category | flops | bytes accessed | tf_op | source)
XLA Modules:
  0.0 550.5 jit_solution(17672893901105111063)
XLA Ops:
  7.2 0.8 copy.113
  8.0 0.8 copy.89
  8.9 0.8 reshape.360
  9.7 36.1 %all-gather = bf16[360448]{0:T(1024)(128)(2,1)S(1)} all-gather(bf16[11264]{0:T(1024)(128)(2,1)S(1)} %pad_maximum_fusion.3), channel_id=2, replica_groups=mesh['grp'=16,'tok'=32] {'tok'}, dimensions={0}, use_global_device_ids=true | all-gather | bytes 743424 | tf_op jit(solution)/shard_map/all_gather | solution.py:49
  45.7 0.3 reshape.407
  46.0 0.2 broadcast_in_dim_reshape.7
  46.3 0.8 copy.90
  48.1 57.2 %all-gather.7.cloned.1.call-done = bf16[16,1024,64]{1,2,0:T(8,128)(2,1)} async-done(((bf16[1,1024,64]{1,2,0:T(8,128)(2,1)}), bf16[16,1024,64]{1,2,0:T(8,128)(2,1)}) %all-gather.7.cloned.1.call-update) | async-done | bytes 2097168 | tf_op jit(solution)/shard_map/all_gather | solution.py:59
  105.3 2.3 convolution_bitcast_fusion.2
  107.6 0.8 copy-done.4
  108.7 0.7 fusion.39
  109.4 0.2 all-gather.11.cloned.1.call-start
  109.7 0.2 broadcast_in_dim_reshape.8
  109.8 0.7 copy.104
  110.7 0.9 slice.81
  111.9 0.5 fusion.11
  112.4 2.4 broadcast_in_dim.44
  114.8 2.6 broadcast_in_dim.49
  117.4 1.3 reshape.366
  118.9 0.9 copy.96
  120.0 9.0 %reduce-window.11 = s32[32,8,128]{2,1,0:T(8,128)S(1)} reduce-window(s32[32,8,128]{2,1,0:T(8,128)S(1)} %fusion.32, s32[]{:T(128)} %constant.34.clone.1), window={size=1x1x128 pad=0_0x0_0x127_0}, to_apply=%region_9.10 | reduce-window | flops 4161536 | bytes 262148 | tf_op jit(solution)/shard_map/reduce-window.1
  130.1 0.7 pad_maximum_fusion
  130.8 1.8 multiply_reduce_fusion
  132.6 50.5 %all-gather.9.cloned.1.call-done = bf16[4096,512]{1,0:T(8,128)(2,1)} async-done(((bf16[128,512]{1,0:T(8,128)(2,1)}), bf16[4096,512]{1,0:T(8,128)(2,1)}) %all-gather.9.cloned.1.call-update) | async-done | bytes 4194320 | tf_op jit(solution)/shard_map/all_gather | solution.py:145
  183.1 3.8 fusion.40
  186.9 2.9 copy.101
  189.8 2.9 copy.99
  192.8 3.5 fusion
  196.3 4.6 fusion.1
  200.9 1.7 copy-done
  202.6 0.5 fusion.12
  203.2 11.2 %fusion.3 = f32[4,256,64]{1,2,0:T(8,128)} fusion(bf16[4,4096,64]{1,2,0:T(8,128)(2,1)} %bitcast.104, f32[4,256,4096]{2,1,0:T(8,128)} %copy-done, f32[4,256]{1,0:T(4,128)S(1)} %get-tuple-element.15, pred[256,4096]{1,0:T(8,128)(4,1)S(1)} %broadcast_in_dim.49), kind=kOutput, calls=%fused_computation.8 | convolution fusion | flops 553648128 | bytes 20189184 | tf_op jit(solution)/shard_map/kqn,knd->kqd/dot_general | solution.py:85
  214.5 1.6 fusion.21
  216.4 24.7 %all-gather.11.cloned.1.call-done = bf16[16,1024,32]{1,2,0:T(8,128)(2,1)} async-done(((bf16[1,1024,32]{1,2,0:T(8,128)(2,1)}), bf16[16,1024,32]{1,2,0:T(8,128)(2,1)}) %all-gather.11.cloned.1.call-update) | async-done | bytes 1048592 | tf_op jit(solution)/shard_map/all_gather | solution.py:59
  241.1 1.6 multiply_reduce_fusion.1
  242.8 14.7 %scatter_custom_fusion = bf16[1280,1024]{1,0:T(8,128)(2,1)} fusion(s32[1024]{0:T(1024)S(1)} %bitcast.118, bf16[128,1024]{1,0:T(8,128)(2,1)S(1)} %multiply_convert_fusion, s32[1024]{0:T(1024)S(1)} %broadcast_clamp_fusion.1, bf16[]{:T(256)} %constant.67.clone.1), kind=kCustom, calls=%fused_computation.17 | custom fusion | bytes 2621442 | tf_op jit(solution)/shard_map/scatter | solution.py:174
  257.6 12.8 %all-to-all-start = ((bf16[32,40,1024]{2,1,0:T(8,128)(2,1)}), bf16[32,40,1024]{2,1,0:T(8,128)(2,1)S(1)}, u32[]{:S(2)}, u32[]{:S(2)}) async-start(bf16[32,40,1024]{2,1,0:T(8,128)(2,1)} %bitcast.34), calls=%async_computation | async-start | bytes 5242880 | tf_op jit(solution)/shard_map/all_to_all | solution.py:176
  270.5 0.5 all-gather.13.cloned.1.call-update
  271.0 0.5 all-gather.15.cloned.1.call-update
  271.6 61.4 %all-gather.13.cloned.1.call-done = bf16[1,1024,1024]{2,1,0:T(8,128)(2,1)} async-done(((bf16[1,64,1024]{2,1,0:T(8,128)(2,1)}), bf16[1,1024,1024]{2,1,0:T(8,128)(2,1)}) %all-gather.13.cloned.1.call-update) | async-done | bytes 2097168 | tf_op jit(solution)/shard_map/all_gather | solution.py:183
  332.9 60.2 %all-to-all-done = bf16[32,40,1024]{2,1,0:T(8,128)(2,1)S(1)} async-done(((bf16[32,40,1024]{2,1,0:T(8,128)(2,1)}), bf16[32,40,1024]{2,1,0:T(8,128)(2,1)S(1)}, u32[]{:S(2)}, u32[]{:S(2)}) %all-to-all-start) | async-done | bytes 2621472 | tf_op jit(solution)/shard_map/all_to_all | solution.py:176
  393.1 6.2 %convolution_bitcast_fusion = f32[1,1280,1024]{2,1,0:T(8,128)} fusion(bf16[1280,1024]{1,0:T(8,128)(2,1)S(1)} %bitcast.102, bf16[1,1024,1024]{2,1,0:T(8,128)(2,1)} %all-gather.13.cloned.1.call-done), kind=kOutput, calls=%fused_computation.10 | convolution fusion | flops 2684354560 | bytes 9961472 | tf_op jit(solution)/shard_map/erd,edf->erf/dot_general | solution.py:180
  399.3 5.9 %convolution_convert_fusion = bf16[1280,1024]{1,0:T(8,128)(2,1)} fusion(f32[1,1280,1024]{2,1,0:T(8,128)} %convolution_bitcast_fusion, bf16[1,512,1024]{2,1,0:T(8,128)(2,1)} %all-gather.15.cloned.1.call-done), kind=kOutput, calls=%fused_computation.13 | convolution fusion | flops 1347420160 | bytes 8912896 | tf_op jit(solution)/shard_map/erf,efd->erd/dot_general | solution.py:188
  405.2 6.9 %all-to-all-start.1 = ((bf16[32,40,1024]{2,1,0:T(8,128)(2,1)}), bf16[32,40,1024]{2,1,0:T(8,128)(2,1)S(1)}, u32[]{:S(2)}, u32[]{:S(2)}) async-start(bf16[32,40,1024]{2,1,0:T(8,128)(2,1)} %bitcast.103), calls=%async_computation.1 | async-start | bytes 5242880 | tf_op jit(solution)/shard_map/all_to_all | solution.py:194
  412.3 122.6 %all-to-all-done.1 = bf16[32,40,1024]{2,1,0:T(8,128)(2,1)S(1)} async-done(((bf16[32,40,1024]{2,1,0:T(8,128)(2,1)}), bf16[32,40,1024]{2,1,0:T(8,128)(2,1)S(1)}, u32[]{:S(2)}, u32[]{:S(2)}) %all-to-all-start.1) | async-done | bytes 2621472 | tf_op jit(solution)/shard_map/all_to_all | solution.py:194
  534.9 5.4 gather_fusion
  540.2 2.9 fusion.6
  543.2 0.8 fusion.27
  (85 shorter events, 3.8 us)
Async XLA Ops:
  7.2 40.0 %copy-start.2 = (bf16[1,128,1024]{2,1,0:T(8,128)(2,1)S(1)}, bf16[1,128,1024]{2,1,0:T(8,128)(2,1)}, u32[]{:S(2)}) copy-start(bf16[1,128,1024]{2,1,0:T(8,128)(2,1)} %param.11) | copy-start | bytes 786436
  7.2 40.1 %copy-start.8 = (f32[1024]{0:T(1024)S(1)}, f32[1024]{0:T(1024)}, u32[]{:S(2)}) copy-start(f32[1024]{0:T(1024)} %param.16) | copy-start | bytes 12292
  7.2 40.2 %copy-start.10 = (s32[1,3]{1,0:T(1,128)S(1)}, s32[1,3]{1,0:T(1,128)}, u32[]{:S(2)}) copy-start(s32[1,3]{1,0:T(1,128)} %param.12) | copy-start | bytes 40
  7.2 98.1 %all-gather.7.cloned.1.call-start = ((), (), s32[]{:S(2)}) async-start(), calls=%async_computation.2 | async-start | bytes 2228224 | tf_op jit(solution)/shard_map/all_gather | solution.py:59
  47.1 136.0 %all-gather.9.cloned.1.call-start = ((), (), s32[]{:S(2)}) async-start(), calls=%async_computation.3 | async-start | bytes 4325376 | tf_op jit(solution)/shard_map/all_gather | solution.py:145
  105.3 6.3 %copy-start.6 = (s32[1,128,8]{1,2,0:T(8,128)S(1)}, s32[1,128,8]{1,2,0:T(8,128)}, u32[]{:S(2)}) copy-start(s32[1,128,8]{1,2,0:T(8,128)} %param.14) | copy-start | bytes 12292
  107.6 0.8 copy-start.4
  109.4 131.6 %all-gather.11.cloned.1.call-start = ((), (), s32[]{:S(2)}) async-start(), calls=%async_computation.4 | async-start | bytes 1114112 | tf_op jit(solution)/shard_map/all_gather | solution.py:59
  117.4 12.2 %slice-start = ((f32[128,1024]{1,0:T(8,128)}), f32[128,512]{1,0:T(8,128)S(1)}, s32[]{:S(2)}) async-start(f32[128,1024]{1,0:T(8,128)} %copy-done.4), calls=%async_computation.7 | async-start | bytes 524288 | tf_op jit(solution)/shard_map/slice | solution.py:124
  196.2 6.4 %copy-start = (f32[4,256,4096]{2,1,0:T(8,128)}, f32[4,256,4096]{2,1,0:T(8,128)S(1)}, u32[]{:S(2)}) copy-start(f32[4,256,4096]{2,1,0:T(8,128)S(1)} %get-tuple-element.22) | copy-start | bytes 50331652
  196.3 6.4 %copy-start.1 = (f32[4,256,512]{2,1,0:T(8,128)S(1)}, f32[4,256,512]{2,1,0:T(8,128)}, u32[]{:S(2)}) copy-start(f32[4,256,512]{2,1,0:T(8,128)} %get-tuple-element.20) | copy-start | bytes 6291460
  203.2 11.2 %copy-start.5 = (bf16[512,256]{0,1:T(8,128)(2,1)S(1)}, bf16[512,256]{0,1:T(8,128)(2,1)}, u32[]{:S(2)}) copy-start(bf16[512,256]{0,1:T(8,128)(2,1)} %copy.96) | copy-start | bytes 786436
  214.5 26.6 %copy-start.3 = (bf16[1,128,1024]{2,1,0:T(8,128)(2,1)S(1)}, bf16[1,128,1024]{2,1,0:T(8,128)(2,1)}, u32[]{:S(2)}) copy-start(bf16[1,128,1024]{2,1,0:T(8,128)(2,1)} %param.11) | copy-start | bytes 786436
  214.5 28.3 %copy-start.7 = (f32[1024]{0:T(1024)S(1)}, f32[1024]{0:T(1024)}, u32[]{:S(2)}) copy-start(f32[1024]{0:T(1024)} %param.19) | copy-start | bytes 12292
  257.6 135.5 %all-to-all-start = ((bf16[32,40,1024]{2,1,0:T(8,128)(2,1)}), bf16[32,40,1024]{2,1,0:T(8,128)(2,1)S(1)}, u32[]{:S(2)}, u32[]{:S(2)}) async-start(bf16[32,40,1024]{2,1,0:T(8,128)(2,1)} %bitcast.34), calls=%async_computation | async-start | bytes 5242880 | tf_op jit(solution)/shard_map/all_to_all | solution.py:176
  270.4 62.5 %all-gather.13.cloned.1.call-start = ((), (), s32[]{:S(2)}) async-start(), calls=%async_computation.5 | async-start | bytes 2228224 | tf_op jit(solution)/shard_map/all_gather | solution.py:183
  271.0 128.3 %all-gather.15.cloned.1.call-start = ((), (), s32[]{:S(2)}) async-start(), calls=%async_computation.6 | async-start | bytes 1114112 | tf_op jit(solution)/shard_map/all_gather | solution.py:191
  405.2 6.9 %copy-start.9 = (f32[1,128,8]{1,2,0:T(8,128)S(1)}, f32[1,128,8]{1,2,0:T(8,128)}, u32[]{:S(2)}) copy-start(f32[1,128,8]{1,2,0:T(8,128)} %param.15) | copy-start | bytes 12292
  405.2 129.7 %all-to-all-start.1 = ((bf16[32,40,1024]{2,1,0:T(8,128)(2,1)}), bf16[32,40,1024]{2,1,0:T(8,128)(2,1)S(1)}, u32[]{:S(2)}, u32[]{:S(2)}) async-start(bf16[32,40,1024]{2,1,0:T(8,128)(2,1)} %bitcast.103), calls=%async_computation.1 | async-start | bytes 5242880 | tf_op jit(solution)/shard_map/all_to_all | solution.py:194
Sparse Core Ops, SparseCore 0:
  47.2 58.0 all-gather.6
  109.5 73.5 all-gather.8
  186.1 54.9 all-gather.10
  273.9 58.9 all-gather.12
  335.8 57.4 all-gather.14
where the time goes:
time: 551 us; the launch traced here: 550 us
  waiting for transfers between devices  378 us (69%)
  local copies, waits for them, and re-layouts  47.2 us (9%)
  blocking collectives  36.1 us (7%)
  matrix products  34.1 us (6%)
  other arithmetic  21 us (4%)
  starting transfers between devices  20.1 us (4%)
  between operations  14.3 us (3%)
    all_to_all x1, waiting for transfers between devices, local(): lax.all_to_all(expert_result.reshape(EXPERTS, CAP, model_width), 'tok', s...  123 us
    all_gather x2, waiting for transfers between devices, gather_rows(): return lax.all_gather(by_columns[None], 'grp', axis=0, tiled=True)  81.9 us
    all_gather x1, waiting for transfers between devices, local(): lax.all_gather(expert_gate_up, 'grp', axis=1, tiled=True)  61.4 us
    all_to_all x1, waiting for transfers between devices, local(): lax.all_to_all(outgoing.reshape(EXPERTS, CAP, model_width), 'tok', split_...  60.2 us
    all_gather x1, waiting for transfers between devices, local(): piece = lax.all_gather(suffix_cache, 'tok', axis=0, tiled=True)  50.5 us
    all_gather x1, blocking collectives, gather_small(): gathered = lax.all_gather(flat[None], 'tok', axis=0, tiled=True)  36.1 us
    scatter x1, local copies, waits for them, and re-layouts, local(): outgoing = jnp.zeros((EXPERTS * CAP, model_width), jnp.bfloat16).at[slot_...  14.7 us
    dot_general x2, matrix products, attend(): jnp.einsum('kqn,knd->kqd', probs.astype(jnp.bfloat16), value_heads, prefe...  12.8 us
  transfers between devices with their start and end apart: 7, of which 6 were waited for; matrix products, arithmetic and copies ran while one was open for 11% of the time, Pallas kernels for 0%

commit v1 on v0

--- a/solution.py
+++ b/solution.py
@@ -16,6 +16,27 @@
 big_negative = -1e30
 
 
+def gather_around(value, axis, dim):
+    size, here, rows = (lax.axis_size(axis), lax.axis_index(axis), value.shape[dim])
+    right = [(i, (i + 1) % size) for i in range(size)]
+    downward = [(i, (i - 1) % size) for i in range(size)]
+    whole = jnp.zeros((*value.shape[:dim], size * rows, *value.shape[dim + 1 :]), value.dtype)
+    whole = lax.dynamic_update_slice_in_dim(whole, value, here * rows, axis=dim)
+    from_left = from_right = value
+    middle = size // 2
+    for lap in range(1, middle + 1):
+        from_left = lax.ppermute(from_left, axis, right)
+        whole = lax.dynamic_update_slice_in_dim(
+            whole, from_left, (here - lap) % size * rows, axis=dim
+        )
+        if lap < size - middle:
+            from_right = lax.ppermute(from_right, axis, downward)
+            whole = lax.dynamic_update_slice_in_dim(
+                whole, from_right, (here + lap) % size * rows, axis=dim
+            )
+    return whole
+
+
 def rms_scale(values, gain):
     values = values.astype(jnp.float32)
     mean_square = jnp.mean(values * values, axis=-1, keepdims=True)
@@ -56,7 +77,7 @@
 
 
 def gather_rows(by_columns):
-    return lax.all_gather(by_columns[None], "grp", axis=0, tiled=True)
+    return gather_around(by_columns[None], "grp", 0)
 
 
 def attend(carry, grouped, keys_values, allowed):

time: 551 us -> 629 us (1.14); the launches traced: 550 us -> 619 us
  starting transfers between devices: 20.1 us -> 149 us
  waiting for transfers between devices: 378 us -> 296 us
  local copies, waits for them, and re-layouts: 47.2 us -> 67.1 us
    ppermute x0 -> x30, starting transfers between devices: none -> 136 us  [the longest x14 103 us: gather_around(): from_right = lax.ppermute(from_right, axis, downward)]
    all_gather x2 -> x0, waiting for transfers between devices: 81.9 us -> none  [gather_rows(): return lax.all_gather(by_columns[None], 'grp', axis=0, tiled=True)]
    all_gather x1, waiting for transfers between devices: 50.5 us -> 0.01 us  [local(): piece = lax.all_gather(suffix_cache, 'tok', axis=0, tiled=True)]
    ppermute x0 -> x30, waiting for transfers between devices: none -> 50.4 us  [the longest x16 40.6 us: gather_around(): from_left = lax.ppermute(from_left, axis, right)]
    ppermute x0 -> x30, local copies, waits for them, and re-layouts: none -> 18.7 us  [the longest x14 10.2 us: gather_around(): from_right = lax.ppermute(from_right, axis, downward)]
  transfers between devices with their start and end apart: 7 -> 35, of which waited for: 6 -> 22; matrix products, arithmetic and copies ran while one was open for 11% -> 8% of each run, Pallas kernels for 0% -> 0%
where the time goes in v1:
time: 629 us; the launch traced here: 619 us
  waiting for transfers between devices  296 us (47%)
  starting transfers between devices  149 us (24%)
  local copies, waits for them, and re-layouts  67.1 us (11%)
  blocking collectives  36.1 us (6%)
  matrix products  30.4 us (5%)
  other arithmetic  22.8 us (4%)
  between operations  17.4 us (3%)
    all_to_all x1, waiting for transfers between devices, local(): lax.all_to_all(expert_result.reshape(EXPERTS, CAP, model_width), 'tok', s...  123 us
    ppermute x14, starting transfers between devices, gather_around(): from_right = lax.ppermute(from_right, axis, downward)  103 us
    all_to_all x1, waiting for transfers between devices, local(): lax.all_to_all(outgoing.reshape(EXPERTS, CAP, model_width), 'tok', split_...  63 us
    all_gather x1, waiting for transfers between devices, local(): lax.all_gather(expert_gate_up, 'grp', axis=1, tiled=True)  58.6 us
    ppermute x16, waiting for transfers between devices, gather_around(): from_left = lax.ppermute(from_left, axis, right)  40.6 us
    all_gather x1, blocking collectives, gather_small(): gathered = lax.all_gather(flat[None], 'tok', axis=0, tiled=True)  36.1 us
    ppermute x16, starting transfers between devices, gather_around(): from_left = lax.ppermute(from_left, axis, right)  32.6 us
    scatter x1, local copies, waits for them, and re-layouts, local(): outgoing = jnp.zeros((EXPERTS * CAP, model_width), jnp.bfloat16).at[slot_...  14.9 us
  transfers between devices with their start and end apart: 35, of which 22 were waited for; matrix products, arithmetic and copies ran while one was open for 8% of the time, Pallas kernels for 0%

profile of v1, /device:TPU:32, one launch (start us, length us, event | category | flops | bytes accessed | tf_op | source)
XLA Modules:
  0.0 618.7 jit_solution(13064849881747171297)
XLA Ops:
  10.5 36.1 %all-gather = bf16[360448]{0:T(1024)(128)(2,1)S(1)} all-gather(bf16[11264]{0:T(1024)(128)(2,1)S(1)} %pad_maximum_fusion.3), channel_id=2, replica_groups=mesh['grp'=16,'tok'=32] {'tok'}, dimensions={0}, use_global_device_ids=true | all-gather | bytes 743424 | tf_op jit(solution)/shard_map/all_gather | solution.py:70
  47.1 3.4 collective-permute-start
  50.5 5.8 collective-permute-start.1
  58.7 2.5 collective-permute-done
  65.3 7.2 %collective-permute-start.3 = (bf16[1,1024,64]{2,1,0:T(8,128)(2,1)}, bf16[1,1024,64]{2,1,0:T(8,128)(2,1)S(1)}, u32[]{:S(2)}, u32[]{:S(2)}) collective-permute-start(bf16[1,1024,64]{2,1,0:T(8,128)(2,1)} %collective-permute-done.1), channel_id=1, source_target_pairs={{0,480},{32,0},{64,32},{96,64},{128,96},{160,128},{192,160},{224,1... | collective-permute-start | bytes 393224 | tf_op jit(solution)/shard_map/ppermute | solution.py:33
  72.5 3.1 collective-permute-done.2
  78.8 7.2 %collective-permute-start.5 = (bf16[1,1024,64]{2,1,0:T(8,128)(2,1)S(1)}, bf16[1,1024,64]{2,1,0:T(8,128)(2,1)}, u32[]{:S(2)}, u32[]{:S(2)}) collective-permute-start(bf16[1,1024,64]{2,1,0:T(8,128)(2,1)S(1)} %collective-permute-done.3), channel_id=1, source_target_pairs={{0,480},{32,0},{64,32},{96,64},{128,96},{160,128},{192,160},{224,1... | collective-permute-start | bytes 393224 | tf_op jit(solution)/shard_map/ppermute | solution.py:33
  86.1 3.1 collective-permute-done.4
  92.4 7.2 %collective-permute-start.7 = (bf16[1,1024,64]{2,1,0:T(8,128)(2,1)}, bf16[1,1024,64]{2,1,0:T(8,128)(2,1)}, u32[]{:S(2)}, u32[]{:S(2)}) collective-permute-start(bf16[1,1024,64]{2,1,0:T(8,128)(2,1)} %collective-permute-done.5), channel_id=1, source_target_pairs={{0,480},{32,0},{64,32},{96,64},{128,96},{160,128},{192,160},{224,1... | collective-permute-start | bytes 393224 | tf_op jit(solution)/shard_map/ppermute | solution.py:33
  105.2 7.5 %collective-permute-start.9 = (bf16[1,1024,64]{2,1,0:T(8,128)(2,1)}, bf16[1,1024,64]{2,1,0:T(8,128)(2,1)}, u32[]{:S(2)}, u32[]{:S(2)}) collective-permute-start(bf16[1,1024,64]{2,1,0:T(8,128)(2,1)} %collective-permute-done.7), channel_id=1, source_target_pairs={{0,480},{32,0},{64,32},{96,64},{128,96},{160,128},{192,160},{224,1... | collective-permute-start | bytes 393224 | tf_op jit(solution)/shard_map/ppermute | solution.py:33
  114.8 2.1 collective-permute-start.10
  117.9 7.7 %collective-permute-start.11 = (bf16[1,1024,64]{2,1,0:T(8,128)(2,1)}, bf16[1,1024,64]{2,1,0:T(8,128)(2,1)}, u32[]{:S(2)}, u32[]{:S(2)}) collective-permute-start(bf16[1,1024,64]{2,1,0:T(8,128)(2,1)} %collective-permute-done.9), channel_id=1, source_target_pairs={{0,480},{32,0},{64,32},{96,64},{128,96},{160,128},{192,160},{224,1... | collective-permute-start | bytes 393224 | tf_op jit(solution)/shard_map/ppermute | solution.py:33
  130.9 7.7 %collective-permute-start.13 = (bf16[1,1024,64]{2,1,0:T(8,128)(2,1)}, bf16[1,1024,64]{2,1,0:T(8,128)(2,1)}, u32[]{:S(2)}, u32[]{:S(2)}) collective-permute-start(bf16[1,1024,64]{2,1,0:T(8,128)(2,1)} %collective-permute-done.11), channel_id=1, source_target_pairs={{0,480},{32,0},{64,32},{96,64},{128,96},{160,128},{192,160},{224,1... | collective-permute-start | bytes 393224 | tf_op jit(solution)/shard_map/ppermute | solution.py:33
  143.9 8.8 %collective-permute-done.14 = bf16[1,1024,64]{2,1,0:T(8,128)(2,1)} collective-permute-done((bf16[1,1024,64]{2,1,0:T(8,128)(2,1)}, bf16[1,1024,64]{2,1,0:T(8,128)(2,1)}, u32[]{:S(2)}, u32[]{:S(2)}) %collective-permute-start.14) | collective-permute-done | bytes 131104 | tf_op jit(solution)/shard_map/ppermute | solution.py:28
  158.6 7.2 %collective-permute-start.16 = (bf16[1,1024,32]{2,1,0:T(8,128)(2,1)S(1)}, bf16[1,1024,32]{2,1,0:T(8,128)(2,1)}, u32[]{:S(2)}, u32[]{:S(2)}) collective-permute-start(bf16[1,1024,32]{2,1,0:T(8,128)(2,1)S(1)} %broadcast_in_dim_reshape.8), channel_id=1, source_target_pairs={{0,480},{32,0},{64,32},{96,64},{128,96},{160,128},{192,160},{224,1... | collective-permute-start | bytes 196616 | tf_op jit(solution)/shard_map/ppermute | solution.py:33
  167.7 2.4 broadcast_in_dim.53
  170.1 2.6 broadcast_in_dim.54
  175.2 9.0 %reduce-window.11 = s32[32,8,128]{2,1,0:T(8,128)S(1)} reduce-window(s32[32,8,128]{2,1,0:T(8,128)S(1)} %fusion.32, s32[]{:T(128)} %constant.178.clone.1), window={size=1x1x128 pad=0_0x0_0x127_0}, to_apply=%region_9.10 | reduce-window | flops 4161536 | bytes 262148 | tf_op jit(solution)/shard_map/reduce-window.1
  190.2 7.3 %collective-permute-start.18 = (bf16[1,1024,32]{2,1,0:T(8,128)(2,1)}, bf16[1,1024,32]{2,1,0:T(8,128)(2,1)S(1)}, u32[]{:S(2)}, u32[]{:S(2)}) collective-permute-start(bf16[1,1024,32]{2,1,0:T(8,128)(2,1)} %collective-permute-done.16), channel_id=1, source_target_pairs={{0,480},{32,0},{64,32},{96,64},{128,96},{160,128},{192,160},{224,1... | collective-permute-start | bytes 196616 | tf_op jit(solution)/shard_map/ppermute | solution.py:33
  197.5 3.1 collective-permute-done.17
  203.7 7.6 %collective-permute-start.20 = (bf16[1,1024,32]{2,1,0:T(8,128)(2,1)S(1)}, bf16[1,1024,32]{2,1,0:T(8,128)(2,1)S(1)}, u32[]{:S(2)}, u32[]{:S(2)}) collective-permute-start(bf16[1,1024,32]{2,1,0:T(8,128)(2,1)S(1)} %collective-permute-done.18), channel_id=1, source_target_pairs={{0,480},{32,0},{64,32},{96,64},{128,96},{160,128},{192,160},{224,1... | collective-permute-start | bytes 196616 | tf_op jit(solution)/shard_map/ppermute | solution.py:33
  211.3 3.7 collective-permute-done.19
  217.8 7.7 %collective-permute-start.22 = (bf16[1,1024,32]{2,1,0:T(8,128)(2,1)S(1)}, bf16[1,1024,32]{2,1,0:T(8,128)(2,1)}, u32[]{:S(2)}, u32[]{:S(2)}) collective-permute-start(bf16[1,1024,32]{2,1,0:T(8,128)(2,1)S(1)} %collective-permute-done.20), channel_id=1, source_target_pairs={{0,480},{32,0},{64,32},{96,64},{128,96},{160,128},{192,160},{224,1... | collective-permute-start | bytes 196616 | tf_op jit(solution)/shard_map/ppermute | solution.py:33
  225.6 3.2 collective-permute-done.21
  228.9 2.1 collective-permute-start.23
  233.2 7.8 %collective-permute-start.24 = (bf16[1,1024,32]{2,1,0:T(8,128)(2,1)}, bf16[1,1024,32]{2,1,0:T(8,128)(2,1)S(1)}, u32[]{:S(2)}, u32[]{:S(2)}) collective-permute-start(bf16[1,1024,32]{2,1,0:T(8,128)(2,1)} %collective-permute-done.22), channel_id=1, source_target_pairs={{0,480},{32,0},{64,32},{96,64},{128,96},{160,128},{192,160},{224,1... | collective-permute-start | bytes 196616 | tf_op jit(solution)/shard_map/ppermute | solution.py:33
  241.9 2.1 collective-permute-start.25
  246.2 7.6 %collective-permute-start.26 = (bf16[1,1024,32]{2,1,0:T(8,128)(2,1)S(1)}, bf16[1,1024,32]{2,1,0:T(8,128)(2,1)}, u32[]{:S(2)}, u32[]{:S(2)}) collective-permute-start(bf16[1,1024,32]{2,1,0:T(8,128)(2,1)S(1)} %collective-permute-done.24), channel_id=1, source_target_pairs={{0,480},{32,0},{64,32},{96,64},{128,96},{160,128},{192,160},{224,1... | collective-permute-start | bytes 196616 | tf_op jit(solution)/shard_map/ppermute | solution.py:33
  255.9 2.8 collective-permute-done.26
  259.8 7.8 %collective-permute-start.28 = (bf16[1,1024,32]{2,1,0:T(8,128)(2,1)}, bf16[1,1024,32]{2,1,0:T(8,128)(2,1)S(1)}, u32[]{:S(2)}, u32[]{:S(2)}) collective-permute-start(bf16[1,1024,32]{2,1,0:T(8,128)(2,1)} %collective-permute-done.26), channel_id=1, source_target_pairs={{0,480},{32,0},{64,32},{96,64},{128,96},{160,128},{192,160},{224,1... | collective-permute-start | bytes 196616 | tf_op jit(solution)/shard_map/ppermute | solution.py:33
  269.7 2.1 collective-permute-done.28
  271.9 7.4 %collective-permute-done.29 = bf16[1,1024,32]{2,1,0:T(8,128)(2,1)S(1)} collective-permute-done((bf16[1,1024,32]{2,1,0:T(8,128)(2,1)S(1)}, bf16[1,1024,32]{2,1,0:T(8,128)(2,1)S(1)}, u32[]{:S(2)}, u32[]{:S(2)}) %collective-permute-start.29) | collective-permute-done | bytes 65568 | tf_op jit(solution)/shard_map/ppermute | solution.py:28
  283.3 3.9 fusion.40
  287.1 2.9 copy.206
  290.0 2.9 copy.204
  292.9 3.5 fusion
  296.5 4.4 fusion.1
  302.2 11.3 %fusion.3 = f32[4,256,64]{1,2,0:T(8,128)} fusion(bf16[4,4096,64]{1,2,0:T(8,128)(2,1)} %bitcast.104, f32[4,256,4096]{2,1,0:T(8,128)} %copy-done, f32[4,256]{1,0:T(4,128)S(1)} %get-tuple-element.15, pred[256,4096]{1,0:T(8,128)(4,1)S(1)} %broadcast_in_dim.54), kind=kOutput, calls=%fused_computation.8 | convolution fusion | flops 553648128 | bytes 20189184 | tf_op jit(solution)/shard_map/kqn,knd->kqd/dot_general | solution.py:106
  316.1 14.9 %scatter_custom_fusion = bf16[1280,1024]{1,0:T(8,128)(2,1)} fusion(s32[1024]{0:T(1024)S(1)} %bitcast.119, bf16[128,1024]{1,0:T(8,128)(2,1)S(1)} %multiply_convert_fusion, s32[1024]{0:T(1024)} %broadcast_clamp_fusion.1, bf16[]{:T(256)} %constant.175.clone.1), kind=kCustom, calls=%fused_computation.17 | custom fusion | bytes 2621952 | tf_op jit(solution)/shard_map/scatter | solution.py:195
  330.9 9.0 %all-to-all-start = ((bf16[32,40,1024]{2,1,0:T(8,128)(2,1)}), bf16[32,40,1024]{2,1,0:T(8,128)(2,1)S(1)}, u32[]{:S(2)}, u32[]{:S(2)}) async-start(bf16[32,40,1024]{2,1,0:T(8,128)(2,1)} %bitcast.34), calls=%async_computation | async-start | bytes 5242880 | tf_op jit(solution)/shard_map/all_to_all | solution.py:197
  341.1 58.6 %all-gather.7.cloned.1.call-done = bf16[1,1024,1024]{2,1,0:T(8,128)(2,1)} async-done(((bf16[1,64,1024]{2,1,0:T(8,128)(2,1)}), bf16[1,1024,1024]{2,1,0:T(8,128)(2,1)}) %all-gather.7.cloned.1.call-update) | async-done | bytes 2097168 | tf_op jit(solution)/shard_map/all_gather | solution.py:204
  399.7 63.0 %all-to-all-done = bf16[32,40,1024]{2,1,0:T(8,128)(2,1)S(1)} async-done(((bf16[32,40,1024]{2,1,0:T(8,128)(2,1)}), bf16[32,40,1024]{2,1,0:T(8,128)(2,1)S(1)}, u32[]{:S(2)}, u32[]{:S(2)}) %all-to-all-start) | async-done | bytes 2621472 | tf_op jit(solution)/shard_map/all_to_all | solution.py:197
  462.6 6.2 convolution_bitcast_fusion
  468.8 5.9 convolution_convert_fusion
  474.7 4.4 all-to-all-start.1
  479.2 122.6 %all-to-all-done.1 = bf16[32,40,1024]{2,1,0:T(8,128)(2,1)S(1)} async-done(((bf16[32,40,1024]{2,1,0:T(8,128)(2,1)}), bf16[32,40,1024]{2,1,0:T(8,128)(2,1)S(1)}, u32[]{:S(2)}, u32[]{:S(2)}) %all-to-all-start.1) | async-done | bytes 2621472 | tf_op jit(solution)/shard_map/all_to_all | solution.py:215
  601.8 5.4 gather_fusion
  607.2 2.9 fusion.6
  (216 shorter events, 76.9 us)
Async XLA Ops:
  8.0 48.3 %copy-start.4 = (bf16[1,128,1024]{2,1,0:T(8,128)(2,1)S(1)}, bf16[1,128,1024]{2,1,0:T(8,128)(2,1)}, u32[]{:S(2)}) copy-start(bf16[1,128,1024]{2,1,0:T(8,128)(2,1)} %param.11) | copy-start | bytes 786436
  8.0 48.5 %copy-start.16 = (s32[1,3]{1,0:T(1,128)S(1)}, s32[1,3]{1,0:T(1,128)}, u32[]{:S(2)}) copy-start(s32[1,3]{1,0:T(1,128)} %param.12) | copy-start | bytes 40
  8.0 275.2 %all-gather.5.cloned.1.call-start = ((), (), s32[]{:S(2)}) async-start(), calls=%async_computation.2 | async-start | bytes 4325376 | tf_op jit(solution)/shard_map/all_gather | solution.py:166
  47.1 14.0 %collective-permute-start = (bf16[1,1024,64]{2,1,0:T(8,128)(2,1)S(1)}, bf16[1,1024,64]{2,1,0:T(8,128)(2,1)}, u32[]{:S(2)}, u32[]{:S(2)}) collective-permute-start(bf16[1,1024,64]{2,1,0:T(8,128)(2,1)S(1)} %broadcast_in_dim_reshape.7), channel_id=1, source_target_pairs={{0,32},{32,64},{64,96},{96,128},{128,160},{160,192},{192,224},{224... | collective-permute-start | bytes 393224 | tf_op jit(solution)/shard_map/ppermute | solution.py:28
  50.5 13.7 %collective-permute-start.1 = (bf16[1,1024,64]{2,1,0:T(8,128)(2,1)S(1)}, bf16[1,1024,64]{2,1,0:T(8,128)(2,1)}, u32[]{:S(2)}, u32[]{:S(2)}) collective-permute-start(bf16[1,1024,64]{2,1,0:T(8,128)(2,1)S(1)} %broadcast_in_dim_reshape.7), channel_id=1, source_target_pairs={{0,480},{32,0},{64,32},{96,64},{128,96},{160,128},{192,160},{224,1... | collective-permute-start | bytes 393224 | tf_op jit(solution)/shard_map/ppermute | solution.py:33
  56.3 2.3 copy-start.14
  57.0 98.5 %copy-start.10 = (f32[128,32]{0,1:T(8,128)}, f32[128,32]{0,1:T(8,128)S(1)}, u32[]{:S(2)}) copy-start(f32[128,32]{0,1:T(8,128)S(1)} %get-tuple-element.18) | copy-start | bytes 49156
  62.2 13.5 %collective-permute-start.2 = (bf16[1,1024,64]{2,1,0:T(8,128)(2,1)}, bf16[1,1024,64]{2,1,0:T(8,128)(2,1)}, u32[]{:S(2)}, u32[]{:S(2)}) collective-permute-start(bf16[1,1024,64]{2,1,0:T(8,128)(2,1)} %collective-permute-done), channel_id=1, source_target_pairs={{0,32},{32,64},{64,96},{96,128},{128,160},{160,192},{192,224},{224... | collective-permute-start | bytes 393224 | tf_op jit(solution)/shard_map/ppermute | solution.py:28
  65.3 13.5 %collective-permute-start.3 = (bf16[1,1024,64]{2,1,0:T(8,128)(2,1)}, bf16[1,1024,64]{2,1,0:T(8,128)(2,1)S(1)}, u32[]{:S(2)}, u32[]{:S(2)}) collective-permute-start(bf16[1,1024,64]{2,1,0:T(8,128)(2,1)} %collective-permute-done.1), channel_id=1, source_target_pairs={{0,480},{32,0},{64,32},{96,64},{128,96},{160,128},{192,160},{224,1... | collective-permute-start | bytes 393224 | tf_op jit(solution)/shard_map/ppermute | solution.py:33
  76.8 12.5 %collective-permute-start.4 = (bf16[1,1024,64]{2,1,0:T(8,128)(2,1)}, bf16[1,1024,64]{2,1,0:T(8,128)(2,1)S(1)}, u32[]{:S(2)}, u32[]{:S(2)}) collective-permute-start(bf16[1,1024,64]{2,1,0:T(8,128)(2,1)} %collective-permute-done.2), channel_id=1, source_target_pairs={{0,32},{32,64},{64,96},{96,128},{128,160},{160,192},{192,224},{224... | collective-permute-start | bytes 393224 | tf_op jit(solution)/shard_map/ppermute | solution.py:28
  78.8 12.5 %collective-permute-start.5 = (bf16[1,1024,64]{2,1,0:T(8,128)(2,1)S(1)}, bf16[1,1024,64]{2,1,0:T(8,128)(2,1)}, u32[]{:S(2)}, u32[]{:S(2)}) collective-permute-start(bf16[1,1024,64]{2,1,0:T(8,128)(2,1)S(1)} %collective-permute-done.3), channel_id=1, source_target_pairs={{0,480},{32,0},{64,32},{96,64},{128,96},{160,128},{192,160},{224,1... | collective-permute-start | bytes 393224 | tf_op jit(solution)/shard_map/ppermute | solution.py:33
  89.4 11.7 %collective-permute-start.6 = (bf16[1,1024,64]{2,1,0:T(8,128)(2,1)S(1)}, bf16[1,1024,64]{2,1,0:T(8,128)(2,1)}, u32[]{:S(2)}, u32[]{:S(2)}) collective-permute-start(bf16[1,1024,64]{2,1,0:T(8,128)(2,1)S(1)} %collective-permute-done.4), channel_id=1, source_target_pairs={{0,32},{32,64},{64,96},{96,128},{128,160},{160,192},{192,224},{224... | collective-permute-start | bytes 393224 | tf_op jit(solution)/shard_map/ppermute | solution.py:28
  92.4 11.7 %collective-permute-start.7 = (bf16[1,1024,64]{2,1,0:T(8,128)(2,1)}, bf16[1,1024,64]{2,1,0:T(8,128)(2,1)}, u32[]{:S(2)}, u32[]{:S(2)}) collective-permute-start(bf16[1,1024,64]{2,1,0:T(8,128)(2,1)} %collective-permute-done.5), channel_id=1, source_target_pairs={{0,480},{32,0},{64,32},{96,64},{128,96},{160,128},{192,160},{224,1... | collective-permute-start | bytes 393224 | tf_op jit(solution)/shard_map/ppermute | solution.py:33
  102.1 11.8 %collective-permute-start.8 = (bf16[1,1024,64]{2,1,0:T(8,128)(2,1)}, bf16[1,1024,64]{2,1,0:T(8,128)(2,1)S(1)}, u32[]{:S(2)}, u32[]{:S(2)}) collective-permute-start(bf16[1,1024,64]{2,1,0:T(8,128)(2,1)} %collective-permute-done.6), channel_id=1, source_target_pairs={{0,32},{32,64},{64,96},{96,128},{128,160},{160,192},{192,224},{224... | collective-permute-start | bytes 393224 | tf_op jit(solution)/shard_map/ppermute | solution.py:28
  105.2 11.7 %collective-permute-start.9 = (bf16[1,1024,64]{2,1,0:T(8,128)(2,1)}, bf16[1,1024,64]{2,1,0:T(8,128)(2,1)}, u32[]{:S(2)}, u32[]{:S(2)}) collective-permute-start(bf16[1,1024,64]{2,1,0:T(8,128)(2,1)} %collective-permute-done.7), channel_id=1, source_target_pairs={{0,480},{32,0},{64,32},{96,64},{128,96},{160,128},{192,160},{224,1... | collective-permute-start | bytes 393224 | tf_op jit(solution)/shard_map/ppermute | solution.py:33
  114.8 39.1 %copy-start.6 = (f32[1,128,1024]{1,2,0:T(8,128)S(1)}, f32[1,128,1024]{1,2,0:T(8,128)}, u32[]{:S(2)}) copy-start(f32[1,128,1024]{1,2,0:T(8,128)} %copy.178) | copy-start | bytes 1572868
  114.8 12.0 %collective-permute-start.10 = (bf16[1,1024,64]{2,1,0:T(8,128)(2,1)}, bf16[1,1024,64]{2,1,0:T(8,128)(2,1)}, u32[]{:S(2)}, u32[]{:S(2)}) collective-permute-start(bf16[1,1024,64]{2,1,0:T(8,128)(2,1)} %copy-done.8), channel_id=1, source_target_pairs={{0,32},{32,64},{64,96},{96,128},{128,160},{160,192},{192,224},{224... | collective-permute-start | bytes 393224 | tf_op jit(solution)/shard_map/ppermute | solution.py:28
  117.9 11.9 %collective-permute-start.11 = (bf16[1,1024,64]{2,1,0:T(8,128)(2,1)}, bf16[1,1024,64]{2,1,0:T(8,128)(2,1)}, u32[]{:S(2)}, u32[]{:S(2)}) collective-permute-start(bf16[1,1024,64]{2,1,0:T(8,128)(2,1)} %collective-permute-done.9), channel_id=1, source_target_pairs={{0,480},{32,0},{64,32},{96,64},{128,96},{160,128},{192,160},{224,1... | collective-permute-start | bytes 393224 | tf_op jit(solution)/shard_map/ppermute | solution.py:33
  127.9 11.9 %collective-permute-start.12 = (bf16[1,1024,64]{2,1,0:T(8,128)(2,1)}, bf16[1,1024,64]{2,1,0:T(8,128)(2,1)}, u32[]{:S(2)}, u32[]{:S(2)}) collective-permute-start(bf16[1,1024,64]{2,1,0:T(8,128)(2,1)} %collective-permute-done.10), channel_id=1, source_target_pairs={{0,32},{32,64},{64,96},{96,128},{128,160},{160,192},{192,224},{224... | collective-permute-start | bytes 393224 | tf_op jit(solution)/shard_map/ppermute | solution.py:28
  130.9 11.9 %collective-permute-start.13 = (bf16[1,1024,64]{2,1,0:T(8,128)(2,1)}, bf16[1,1024,64]{2,1,0:T(8,128)(2,1)}, u32[]{:S(2)}, u32[]{:S(2)}) collective-permute-start(bf16[1,1024,64]{2,1,0:T(8,128)(2,1)} %collective-permute-done.11), channel_id=1, source_target_pairs={{0,480},{32,0},{64,32},{96,64},{128,96},{160,128},{192,160},{224,1... | collective-permute-start | bytes 393224 | tf_op jit(solution)/shard_map/ppermute | solution.py:33
  140.9 11.9 %collective-permute-start.14 = (bf16[1,1024,64]{2,1,0:T(8,128)(2,1)}, bf16[1,1024,64]{2,1,0:T(8,128)(2,1)}, u32[]{:S(2)}, u32[]{:S(2)}) collective-permute-start(bf16[1,1024,64]{2,1,0:T(8,128)(2,1)} %collective-permute-done.12), channel_id=1, source_target_pairs={{0,32},{32,64},{64,96},{96,128},{128,160},{160,192},{192,224},{224... | collective-permute-start | bytes 393224 | tf_op jit(solution)/shard_map/ppermute | solution.py:28
  154.6 12.2 %copy-start.11 = (s32[1,128,8]{1,2,0:T(8,128)S(1)}, s32[1,128,8]{1,2,0:T(8,128)}, u32[]{:S(2)}) copy-start(s32[1,128,8]{1,2,0:T(8,128)} %param.14) | copy-start | bytes 12292
  156.6 29.5 %collective-permute-start.15 = (bf16[1,1024,32]{2,1,0:T(8,128)(2,1)S(1)}, bf16[1,1024,32]{2,1,0:T(8,128)(2,1)}, u32[]{:S(2)}, u32[]{:S(2)}) collective-permute-start(bf16[1,1024,32]{2,1,0:T(8,128)(2,1)S(1)} %broadcast_in_dim_reshape.8), channel_id=1, source_target_pairs={{0,32},{32,64},{64,96},{96,128},{128,160},{160,192},{192,224},{224... | collective-permute-start | bytes 196616 | tf_op jit(solution)/shard_map/ppermute | solution.py:28
  158.6 30.5 %collective-permute-start.16 = (bf16[1,1024,32]{2,1,0:T(8,128)(2,1)S(1)}, bf16[1,1024,32]{2,1,0:T(8,128)(2,1)}, u32[]{:S(2)}, u32[]{:S(2)}) collective-permute-start(bf16[1,1024,32]{2,1,0:T(8,128)(2,1)S(1)} %broadcast_in_dim_reshape.8), channel_id=1, source_target_pairs={{0,480},{32,0},{64,32},{96,64},{128,96},{160,128},{192,160},{224,1... | collective-permute-start | bytes 196616 | tf_op jit(solution)/shard_map/ppermute | solution.py:33
  187.2 13.4 %collective-permute-start.17 = (bf16[1,1024,32]{2,1,0:T(8,128)(2,1)}, bf16[1,1024,32]{2,1,0:T(8,128)(2,1)S(1)}, u32[]{:S(2)}, u32[]{:S(2)}) collective-permute-start(bf16[1,1024,32]{2,1,0:T(8,128)(2,1)} %collective-permute-done.15), channel_id=1, source_target_pairs={{0,32},{32,64},{64,96},{96,128},{128,160},{160,192},{192,224},{224... | collective-permute-start | bytes 196616 | tf_op jit(solution)/shard_map/ppermute | solution.py:28
  190.2 13.4 %collective-permute-start.18 = (bf16[1,1024,32]{2,1,0:T(8,128)(2,1)}, bf16[1,1024,32]{2,1,0:T(8,128)(2,1)S(1)}, u32[]{:S(2)}, u32[]{:S(2)}) collective-permute-start(bf16[1,1024,32]{2,1,0:T(8,128)(2,1)} %collective-permute-done.16), channel_id=1, source_target_pairs={{0,480},{32,0},{64,32},{96,64},{128,96},{160,128},{192,160},{224,1... | collective-permute-start | bytes 196616 | tf_op jit(solution)/shard_map/ppermute | solution.py:33
  200.7 14.3 %collective-permute-start.19 = (bf16[1,1024,32]{2,1,0:T(8,128)(2,1)S(1)}, bf16[1,1024,32]{2,1,0:T(8,128)(2,1)S(1)}, u32[]{:S(2)}, u32[]{:S(2)}) collective-permute-start(bf16[1,1024,32]{2,1,0:T(8,128)(2,1)S(1)} %collective-permute-done.17), channel_id=1, source_target_pairs={{0,32},{32,64},{64,96},{96,128},{128,160},{160,192},{192,224},{224... | collective-permute-start | bytes 196616 | tf_op jit(solution)/shard_map/ppermute | solution.py:28
  203.7 14.0 %collective-permute-start.20 = (bf16[1,1024,32]{2,1,0:T(8,128)(2,1)S(1)}, bf16[1,1024,32]{2,1,0:T(8,128)(2,1)S(1)}, u32[]{:S(2)}, u32[]{:S(2)}) collective-permute-start(bf16[1,1024,32]{2,1,0:T(8,128)(2,1)S(1)} %collective-permute-done.18), channel_id=1, source_target_pairs={{0,480},{32,0},{64,32},{96,64},{128,96},{160,128},{192,160},{224,1... | collective-permute-start | bytes 196616 | tf_op jit(solution)/shard_map/ppermute | solution.py:33
  215.1 13.7 %collective-permute-start.21 = (bf16[1,1024,32]{2,1,0:T(8,128)(2,1)S(1)}, bf16[1,1024,32]{2,1,0:T(8,128)(2,1)S(1)}, u32[]{:S(2)}, u32[]{:S(2)}) collective-permute-start(bf16[1,1024,32]{2,1,0:T(8,128)(2,1)S(1)} %collective-permute-done.19), channel_id=1, source_target_pairs={{0,32},{32,64},{64,96},{96,128},{128,160},{160,192},{192,224},{224... | collective-permute-start | bytes 196616 | tf_op jit(solution)/shard_map/ppermute | solution.py:28
  217.8 14.4 %collective-permute-start.22 = (bf16[1,1024,32]{2,1,0:T(8,128)(2,1)S(1)}, bf16[1,1024,32]{2,1,0:T(8,128)(2,1)}, u32[]{:S(2)}, u32[]{:S(2)}) collective-permute-start(bf16[1,1024,32]{2,1,0:T(8,128)(2,1)S(1)} %collective-permute-done.20), channel_id=1, source_target_pairs={{0,480},{32,0},{64,32},{96,64},{128,96},{160,128},{192,160},{224,1... | collective-permute-start | bytes 196616 | tf_op jit(solution)/shard_map/ppermute | solution.py:33
  228.9 50.5 %slice-start = ((f32[128,1024]{1,0:T(8,128)}), f32[128,512]{1,0:T(8,128)S(1)}, s32[]{:S(2)}) async-start(f32[128,1024]{1,0:T(8,128)} %copy-done.7), calls=%async_computation.5 | async-start | bytes 524288 | tf_op jit(solution)/shard_map/slice | solution.py:145
  228.9 12.9 %collective-permute-start.23 = (bf16[1,1024,32]{2,1,0:T(8,128)(2,1)S(1)}, bf16[1,1024,32]{2,1,0:T(8,128)(2,1)S(1)}, u32[]{:S(2)}, u32[]{:S(2)}) collective-permute-start(bf16[1,1024,32]{2,1,0:T(8,128)(2,1)S(1)} %collective-permute-done.21), channel_id=1, source_target_pairs={{0,32},{32,64},{64,96},{96,128},{128,160},{160,192},{192,224},{224... | collective-permute-start | bytes 196616 | tf_op jit(solution)/shard_map/ppermute | solution.py:28
  233.2 12.8 %collective-permute-start.24 = (bf16[1,1024,32]{2,1,0:T(8,128)(2,1)}, bf16[1,1024,32]{2,1,0:T(8,128)(2,1)S(1)}, u32[]{:S(2)}, u32[]{:S(2)}) collective-permute-start(bf16[1,1024,32]{2,1,0:T(8,128)(2,1)} %collective-permute-done.22), channel_id=1, source_target_pairs={{0,480},{32,0},{64,32},{96,64},{128,96},{160,128},{192,160},{224,1... | collective-permute-start | bytes 196616 | tf_op jit(solution)/shard_map/ppermute | solution.py:33
  241.9 11.9 %collective-permute-start.25 = (bf16[1,1024,32]{2,1,0:T(8,128)(2,1)S(1)}, bf16[1,1024,32]{2,1,0:T(8,128)(2,1)S(1)}, u32[]{:S(2)}, u32[]{:S(2)}) collective-permute-start(bf16[1,1024,32]{2,1,0:T(8,128)(2,1)S(1)} %collective-permute-done.23), channel_id=1, source_target_pairs={{0,32},{32,64},{64,96},{96,128},{128,160},{160,192},{192,224},{224... | collective-permute-start | bytes 196616 | tf_op jit(solution)/shard_map/ppermute | solution.py:28
  246.2 12.5 %collective-permute-start.26 = (bf16[1,1024,32]{2,1,0:T(8,128)(2,1)S(1)}, bf16[1,1024,32]{2,1,0:T(8,128)(2,1)}, u32[]{:S(2)}, u32[]{:S(2)}) collective-permute-start(bf16[1,1024,32]{2,1,0:T(8,128)(2,1)S(1)} %collective-permute-done.24), channel_id=1, source_target_pairs={{0,480},{32,0},{64,32},{96,64},{128,96},{160,128},{192,160},{224,1... | collective-permute-start | bytes 196616 | tf_op jit(solution)/shard_map/ppermute | solution.py:33
  254.0 13.7 %collective-permute-start.27 = (bf16[1,1024,32]{2,1,0:T(8,128)(2,1)S(1)}, bf16[1,1024,32]{2,1,0:T(8,128)(2,1)S(1)}, u32[]{:S(2)}, u32[]{:S(2)}) collective-permute-start(bf16[1,1024,32]{2,1,0:T(8,128)(2,1)S(1)} %collective-permute-done.25), channel_id=1, source_target_pairs={{0,32},{32,64},{64,96},{96,128},{128,160},{160,192},{192,224},{224... | collective-permute-start | bytes 196616 | tf_op jit(solution)/shard_map/ppermute | solution.py:28
  259.8 12.0 %collective-permute-start.28 = (bf16[1,1024,32]{2,1,0:T(8,128)(2,1)}, bf16[1,1024,32]{2,1,0:T(8,128)(2,1)S(1)}, u32[]{:S(2)}, u32[]{:S(2)}) collective-permute-start(bf16[1,1024,32]{2,1,0:T(8,128)(2,1)} %collective-permute-done.26), channel_id=1, source_target_pairs={{0,480},{32,0},{64,32},{96,64},{128,96},{160,128},{192,160},{224,1... | collective-permute-start | bytes 196616 | tf_op jit(solution)/shard_map/ppermute | solution.py:33
  267.7 11.6 %collective-permute-start.29 = (bf16[1,1024,32]{2,1,0:T(8,128)(2,1)S(1)}, bf16[1,1024,32]{2,1,0:T(8,128)(2,1)S(1)}, u32[]{:S(2)}, u32[]{:S(2)}) collective-permute-start(bf16[1,1024,32]{2,1,0:T(8,128)(2,1)S(1)} %collective-permute-done.27), channel_id=1, source_target_pairs={{0,32},{32,64},{64,96},{96,128},{128,160},{160,192},{192,224},{224... | collective-permute-start | bytes 196616 | tf_op jit(solution)/shard_map/ppermute | solution.py:28
  279.5 3.8 copy-start.2
  296.4 5.7 copy-start
  302.2 11.3 %copy-start.1 = (f32[4,256,512]{2,1,0:T(8,128)S(1)}, f32[4,256,512]{2,1,0:T(8,128)}, u32[]{:S(2)}) copy-start(f32[4,256,512]{2,1,0:T(8,128)} %get-tuple-element.20) | copy-start | bytes 6291460
  314.0 1.4 copy-start.3
  314.0 1.4 copy-start.5
  330.9 131.7 %all-to-all-start = ((bf16[32,40,1024]{2,1,0:T(8,128)(2,1)}), bf16[32,40,1024]{2,1,0:T(8,128)(2,1)S(1)}, u32[]{:S(2)}, u32[]{:S(2)}) async-start(bf16[32,40,1024]{2,1,0:T(8,128)(2,1)} %bitcast.34), calls=%async_computation | async-start | bytes 5242880 | tf_op jit(solution)/shard_map/all_to_all | solution.py:197
  339.9 59.8 %all-gather.7.cloned.1.call-start = ((), (), s32[]{:S(2)}) async-start(), calls=%async_computation.3 | async-start | bytes 2228224 | tf_op jit(solution)/shard_map/all_gather | solution.py:204
  340.5 128.3 %all-gather.9.cloned.1.call-start = ((), (), s32[]{:S(2)}) async-start(), calls=%async_computation.4 | async-start | bytes 1114112 | tf_op jit(solution)/shard_map/all_gather | solution.py:212
  474.7 4.4 copy-start.15
  474.7 127.1 %all-to-all-start.1 = ((bf16[32,40,1024]{2,1,0:T(8,128)(2,1)}), bf16[32,40,1024]{2,1,0:T(8,128)(2,1)S(1)}, u32[]{:S(2)}, u32[]{:S(2)}) async-start(bf16[32,40,1024]{2,1,0:T(8,128)(2,1)} %bitcast.103), calls=%async_computation.1 | async-start | bytes 5242880 | tf_op jit(solution)/shard_map/all_to_all | solution.py:215
  (6 other events, 5.2 us)
Sparse Core Ops, SparseCore 0:
  156.6 66.5 all-gather.4
Sparse Core Ops, SparseCore 1:
  343.4 56.2 all-gather.6
  402.5 57.6 all-gather.8
